TPU v7x, 32 devices: a whole 2x2x4 slice. The times are simulated.
32 devices in a mesh: dp: 4 (over z), seq: 8 (over y, x, core).
Axes of the slice: x: 2, y: 2, z: 4, core: 2. Of those that a mesh axis runs over, the one named last changes fastest.
Arguments:
- tokens: float32 [4, 1024, 2048], P('dp', 'seq'), may hold values from -10 to 10, as said below
- cotangent: float32 [4, 1024, 2048], P('dp', 'seq'), may hold values from -6 to 6
- short_weights: float32 [3, 8, 2048], replicated, may hold values from 0.2 to 0.6
Outputs:
- grad_tokens: float32 [4, 1024, 2048], P('dp', 'seq')
- grad_weights: float32 [3, 8, 2048], P(None, None, 'seq')
Inputs may be any that keep to these rules, and one draw needn't show every extreme that they name: `tokens`: Real-valued activations of order one.
All inputs are finite; a program needn't handle non-finite values.
Results may differ from a plain program's by a relative error of at most 0.0003.
Values sent between devices are 32-bit elements; how exact they have to be, the bound alone decides.
No kernel may reach another device: no remote copies, remote signals or barrier semaphores. Data moves between devices by JAX's collectives and lax.ppermute only.
A program may use at most 64 MiB of HBM per device.

v0:
```python
import jax
import jax.numpy as jnp
from jax import lax
from jax.sharding import PartitionSpec as P

HEAD = 64
D = 2048
K = 8


def attend_back(query, key, value, grad_o):
    scale = HEAD ** (-0.5)
    hi = lax.Precision.HIGHEST
    scores = scale * jnp.einsum("qhe,khe->hqk", query, key, precision=hi)
    top = jnp.max(scores, axis=-1, keepdims=True)
    expo = jnp.exp(scores - top)
    probs = expo / jnp.sum(expo, axis=-1, keepdims=True)
    grad_probs = jnp.einsum("qhe,khe->hqk", grad_o, value, precision=hi)
    delta = jnp.sum(probs * grad_probs, axis=-1, keepdims=True)
    grad_scores = probs * (grad_probs - delta)
    grad_q = scale * jnp.einsum("hqk,khe->qhe", grad_scores, key, precision=hi)
    grad_k = scale * jnp.einsum("hqk,qhe->khe", grad_scores, query, precision=hi)
    grad_v = jnp.einsum("hqk,qhe->khe", probs, grad_o, precision=hi)
    return (grad_q, grad_k, grad_v)


def head_backward(query, key, value, grad_o):
    batch, sums, width = query.shape
    heads_here = width // HEAD

    def one_sequence(parts):
        shaped = [p.reshape(sums, heads_here, HEAD) for p in parts]
        grads = attend_back(shaped[0], shaped[1], shaped[2], shaped[3])
        return tuple((g.reshape(sums, width) for g in grads))

    return jax.vmap(one_sequence)((query, key, value, grad_o))


def per_device(tokens, cotangent, short_weights):
    hi = lax.Precision.HIGHEST
    batch = tokens.shape[0]
    col_tokens, col_grad = (
        lax.all_to_all(tokens, "seq", split_axis=2, concat_axis=1, tiled=True),
        lax.all_to_all(cotangent, "seq", split_axis=2, concat_axis=1, tiled=True),
    )
    length = col_tokens.shape[1]
    width = col_tokens.shape[2]
    sums = length // K
    start = lax.axis_index("seq") * width
    local_weights = lax.dynamic_slice_in_dim(short_weights, start, width, 2)
    grouped = col_tokens.reshape(batch, sums, K, width)
    summary = jnp.einsum("bjic,mic->mbjc", grouped, local_weights, precision=hi)
    grad_o = jnp.sum(col_grad.reshape(batch, sums, K, width), axis=2)
    grad_q, grad_k, grad_v = head_backward(summary[0], summary[1], summary[2], grad_o)
    grad_summary = jnp.stack([grad_q, grad_k, grad_v])
    grad_cols = jnp.einsum("mbjc,mic->bjic", grad_summary, local_weights, precision=hi).reshape(
        batch, length, width
    )
    grad_tokens = lax.all_to_all(grad_cols, "seq", split_axis=1, concat_axis=2, tiled=True)
    partial_value = jnp.einsum("mbjc,bjic->mic", grad_summary, grouped, precision=hi)
    raw = lax.psum(partial_value, "dp")
    total_sq = lax.psum(jnp.sum(raw * raw), "seq")
    mean_sq = total_sq / (3 * K * D)
    factor = jnp.minimum(1.0, 1.0 / jnp.sqrt(mean_sq + 1e-06))
    return (grad_tokens, raw * factor)


def solution(mesh):
    return jax.shard_map(
        per_device,
        mesh=mesh,
        in_specs=(P("dp", "seq", None), P("dp", "seq", None), P()),
        out_specs=(P("dp", "seq", None), P(None, None, "seq")),
        check_vma=False,
    )
```

profile of v0, /device:TPU:0, one launch (start us, length us, event | category | flops | bytes accessed | tf_op | source)
XLA Modules:
  0.0 110.5 jit_solution(7120607152902859944)
XLA Ops:
  0.6 0.0 copy-start
  0.6 3.6 %copy.65 = f32[1,128,2048]{1,0,2:T(1,128)} copy(f32[1,128,2048]{2,1,0:T(8,128)} %param.4) | data formatting | bytes 2097152 | tf_op args[1]
  4.3 0.0 copy-start.1
  4.3 5.3 %all-to-all-start.1 = ((f32[1,128,2048]{1,0,2:T(1,128)}), f32[1,128,2048]{1,0,2:T(1,128)S(1)}, u32[]{:S(2)}, u32[]{:S(2)}) async-start(f32[1,128,2048]{1,0,2:T(1,128)} %copy.65), calls=%async_computation.1 | async-start | bytes 2097152 | tf_op jit(solution)/shard_map/all_to_all | solution.py:44
  9.6 0.0 copy-done.1
  9.6 1.9 %copy.62 = f32[1,128,2048]{1,0,2:T(1,128)} copy(f32[1,128,2048]{2,1,0:T(8,128)S(1)} %copy-done.1) | data formatting | bytes 2097152 | tf_op args[0]
  11.5 13.5 %all-to-all-done.1 = f32[1,128,2048]{1,0,2:T(1,128)S(1)} async-done(((f32[1,128,2048]{1,0,2:T(1,128)}), f32[1,128,2048]{1,0,2:T(1,128)S(1)}, u32[]{:S(2)}, u32[]{:S(2)}) %all-to-all-start.1) | async-done | bytes 1048608 | tf_op jit(solution)/shard_map/all_to_all | solution.py:44
  25.0 3.6 %all-to-all-start = ((f32[1,128,2048]{1,0,2:T(1,128)}), f32[1,128,2048]{1,0,2:T(1,128)S(1)}, u32[]{:S(2)}, u32[]{:S(2)}) async-start(f32[1,128,2048]{1,0,2:T(1,128)} %copy.62), calls=%async_computation | async-start | bytes 2097152 | tf_op jit(solution)/shard_map/all_to_all | solution.py:43
  28.6 0.0 copy-done
  28.6 0.2 copy.84
  28.8 1.3 %copy.66 = f32[1,8,128,256]{3,2,1,0:T(8,128)} copy(f32[1,8,128,256]{2,3,1,0:T(8,128)S(1)} %bitcast.64) | data formatting | bytes 2097152 | tf_op jit(solution)/shard_map/all_to_all | solution.py:44
  30.1 1.5 %reduce_sum.37 = f32[128,256]{1,0:T(8,128)S(1)} reduce(f32[128,8,256]{2,1,0:T(8,128)} %bitcast.65, f32[]{:T(128)} %constant.6.clone.1), dimensions={1}, to_apply=%region_2.0 | reduce | flops 229376 | bytes 1179652 | tf_op jit(solution)/shard_map/reduce_sum | solution.py:53
  31.6 0.1 copy.67
  31.7 12.2 %all-to-all-done = f32[1,128,2048]{1,0,2:T(1,128)S(1)} async-done(((f32[1,128,2048]{1,0,2:T(1,128)}), f32[1,128,2048]{1,0,2:T(1,128)S(1)}, u32[]{:S(2)}, u32[]{:S(2)}) %all-to-all-start) | async-done | bytes 1048608 | tf_op jit(solution)/shard_map/all_to_all | solution.py:43
  43.9 0.3 copy.63
  44.2 0.6 copy.64
  44.8 1.8 %convolution_bitcast_fusion.2 = f32[3,1,128,256]{2,0,3,1:T(4,128)S(1)} fusion(f32[3,8,256]{1,0,2:T(4,128)S(1)} %copy.84, f32[128,8,256]{0,1,2:T(8,128)S(1)} %copy.64), kind=kOutput, calls=%fused_computation.2 | convolution fusion | flops 9437184 | bytes 1466368 | tf_op jit(solution)/shard_map/bjic,mic->mbjc/dot_general | solution.py:52
  46.6 0.3 fusion.8
  46.8 0.6 fusion.9
  47.4 0.1 fusion.1
  47.5 0.6 fusion.5
  48.1 0.6 multiply_reduce_fusion.1
  48.7 0.6 convolution_multiply_fusion.1
  49.4 0.0 copy-start.2
  49.4 0.4 convolution_multiply_fusion.2
  49.8 0.0 copy-start.4
  49.8 0.2 copy-done.2
  50.0 0.4 copy-done.4
  50.4 3.4 %convolution_bitcast_fusion = f32[1,128,8,256]{1,2,3,0:T(8,128)} fusion(f32[3,8,256]{1,0,2:T(4,128)S(1)} %copy.84, f32[1,1,128,256]{2,0,3,1:T(1,128)S(1)} %bitcast.74, f32[1,1,128,256]{2,0,3,1:T(1,128)S(1)} %bitcast.76, f32[1,1,128,256]{2,0,3,1:T(1,128)S(1)} %bitcast.78), kind=kOutput, calls=%fused_computation | convolution fusion | flops 9633792 | bytes 1466368 | tf_op jit(solution)/shard_map/mbjc,mic->bjic/dot_general | solution.py:56
  53.8 1.7 %copy.74 = f32[1,128,8,256]{3,2,1,0:T(8,128)S(1)} copy(f32[1,128,8,256]{1,2,3,0:T(8,128)} %convolution_bitcast_fusion) | data formatting | bytes 2097152 | tf_op jit(solution)/shard_map/mbjc,mic->bjic/transpose | solution.py:56
  55.6 2.0 %copy.75 = f32[1,1024,256]{2,0,1:T(1,128)} copy(f32[1,1024,256]{2,1,0:T(8,128)S(1)} %bitcast.67) | data formatting | bytes 2097152 | tf_op jit(solution)/shard_map/reshape | solution.py:56
  57.6 0.0 copy-start.3
  57.6 0.0 copy-start.5
  57.6 3.9 %all-to-all-start.2 = ((f32[1,1024,256]{2,0,1:T(1,128)}), f32[1,1024,256]{2,0,1:T(1,128)S(1)}, u32[]{:S(2)}, u32[]{:S(2)}) async-start(f32[1,1024,256]{2,0,1:T(1,128)} %copy.75), calls=%async_computation.2 | async-start | bytes 2097152 | tf_op jit(solution)/shard_map/all_to_all | solution.py:59
  61.5 0.0 copy-done.3
  61.5 0.0 copy-done.5
  61.5 2.0 %convolution_bitcast_fusion.1 = f32[3,8,256]{1,0,2:T(4,128)S(1)} fusion(f32[128,8,256]{0,1,2:T(8,128)S(1)} %copy.64, f32[1,1,128,256]{2,0,3,1:T(1,128)S(1)} %bitcast.75, f32[1,1,128,256]{2,0,3,1:T(1,128)S(1)} %bitcast.77, f32[1,1,128,256]{2,0,3,1:T(1,128)S(1)} %bitcast.79), kind=kOutput, calls=%fused_computation.1 | convolution fusion | flops 9633792 | bytes 1466368 | tf_op jit(solution)/shard_map/mbjc,bjic->mic/dot_general | solution.py:60
  63.5 30.4 %psum.14 = f32[3,8,256]{1,0,2:T(4,128)S(1)} all-reduce(f32[3,8,256]{1,0,2:T(4,128)S(1)} %convolution_bitcast_fusion.1), channel_id=1, replica_groups=mesh['dp'=4,'seq'=8] {'dp'}, use_global_device_ids=true, to_apply=%region_4.0 | all-reduce | flops 6144 | bytes 49152 | tf_op jit(solution)/shard_map/psum | solution.py:61
  94.0 0.9 multiply_reduce_fusion
  94.8 12.4 %psum.15 = f32[]{:T(128)} all-reduce(f32[]{:T(128)} %multiply_reduce_fusion), channel_id=1, replica_groups=mesh['dp'=4,'seq'=8] {'seq'}, use_global_device_ids=true, to_apply=%region_6.0 | all-reduce | flops 1 | bytes 8 | tf_op jit(solution)/shard_map/psum | solution.py:62
  107.9 0.1 broadcast_multiply_fusion
  108.0 0.8 copy.79
  108.8 0.0 all-to-all-done.2
  108.8 0.1 copy.83
  108.9 0.3 copy.76
  109.2 1.3 %copy.78 = f32[1,128,2048]{2,1,0:T(8,128)} copy(f32[1,128,2048]{1,2,0:T(8,128)S(1)} %bitcast.69) | data formatting | bytes 2097152
  (1 shorter events, 0.0 us)
Async XLA Ops:
  0.6 27.9 %copy-start = (f32[3,8,2048]{2,1,0:T(8,128)S(1)}, f32[3,8,2048]{2,1,0:T(8,128)}, u32[]{:S(2)}) copy-start(f32[3,8,2048]{2,1,0:T(8,128)} %param.5) | copy-start | bytes 589828
  4.3 5.3 %copy-start.1 = (f32[1,128,2048]{2,1,0:T(8,128)S(1)}, f32[1,128,2048]{2,1,0:T(8,128)}, u32[]{:S(2)}) copy-start(f32[1,128,2048]{2,1,0:T(8,128)} %param.3) | copy-start | bytes 3145732
  4.3 20.7 %all-to-all-start.1 = ((f32[1,128,2048]{1,0,2:T(1,128)}), f32[1,128,2048]{1,0,2:T(1,128)S(1)}, u32[]{:S(2)}, u32[]{:S(2)}) async-start(f32[1,128,2048]{1,0,2:T(1,128)} %copy.65), calls=%async_computation.1 | async-start | bytes 2097152 | tf_op jit(solution)/shard_map/all_to_all | solution.py:44
  25.0 18.9 %all-to-all-start = ((f32[1,128,2048]{1,0,2:T(1,128)}), f32[1,128,2048]{1,0,2:T(1,128)S(1)}, u32[]{:S(2)}, u32[]{:S(2)}) async-start(f32[1,128,2048]{1,0,2:T(1,128)} %copy.62), calls=%async_computation | async-start | bytes 2097152 | tf_op jit(solution)/shard_map/all_to_all | solution.py:43
  49.4 0.6 copy-start.2
  49.8 0.7 copy-start.4
  57.6 3.9 %copy-start.3 = (f32[4,64,128]{2,1,0:T(8,128)S(1)}, f32[4,64,128]{2,1,0:T(8,128)}, u32[]{:S(2)}) copy-start(f32[4,64,128]{2,1,0:T(8,128)} %copy-done.2) | copy-start | bytes 393220
  57.6 3.9 %copy-start.5 = (f32[4,64,128]{2,1,0:T(8,128)S(1)}, f32[4,64,128]{2,1,0:T(8,128)}, u32[]{:S(2)}) copy-start(f32[4,64,128]{2,1,0:T(8,128)} %copy-done.4) | copy-start | bytes 393220
  57.6 51.2 %all-to-all-start.2 = ((f32[1,1024,256]{2,0,1:T(1,128)}), f32[1,1024,256]{2,0,1:T(1,128)S(1)}, u32[]{:S(2)}, u32[]{:S(2)}) async-start(f32[1,1024,256]{2,0,1:T(1,128)} %copy.75), calls=%async_computation.2 | async-start | bytes 2097152 | tf_op jit(solution)/shard_map/all_to_all | solution.py:59
where the time goes:
time: 111 us
  blocking collectives  42.8 us (39%)
  waiting for transfers between devices  25.6 us (23%)
  local copies, waits for them, and re-layouts  15.2 us (14%)
  starting transfers between devices  12.8 us (12%)
  matrix products  10 us (9%)
  other arithmetic  2.51 us (2%)
  between operations  1.53 us (1%)
    psum x1, blocking collectives, per_device(): raw = lax.psum(partial_value, 'dp')  30.4 us
    all_to_all x1, waiting for transfers between devices, per_device(): lax.all_to_all(cotangent, 'seq', split_axis=2, concat_axis=1, tiled=True)  13.5 us
    psum x1, blocking collectives, per_device(): total_sq = lax.psum(jnp.sum(raw * raw), 'seq')  12.4 us
    all_to_all x1, waiting for transfers between devices, per_device(): lax.all_to_all(tokens, 'seq', split_axis=2, concat_axis=1, tiled=True)  12.2 us
    unnamed x18, local copies, waits for them, and re-layouts  8.56 us
    all_to_all x1, starting transfers between devices, per_device(): lax.all_to_all(cotangent, 'seq', split_axis=2, concat_axis=1, tiled=True)  5.33 us
    all_to_all x1, starting transfers between devices, per_device(): lax.all_to_all(grad_cols, 'seq', split_axis=1, concat_axis=2, tiled=True)  3.87 us
    all_to_all x1, starting transfers between devices, per_device(): lax.all_to_all(tokens, 'seq', split_axis=2, concat_axis=1, tiled=True)  3.56 us
  transfers between devices with their start and end apart: 3, of which 2 were waited for; matrix products, arithmetic and copies ran while one was open for 8% of the time, Pallas kernels for 0%

commit v1 on v0

--- a/solution.py
+++ b/solution.py
@@ -58,7 +58,7 @@
     )
     grad_tokens = lax.all_to_all(grad_cols, "seq", split_axis=1, concat_axis=2, tiled=True)
     partial_value = jnp.einsum("mbjc,bjic->mic", grad_summary, grouped, precision=hi)
-    raw = lax.psum(partial_value, "dp")
+    raw = jnp.sum(lax.all_gather(partial_value, "dp"), axis=0)
     total_sq = lax.psum(jnp.sum(raw * raw), "seq")
     mean_sq = total_sq / (3 * K * D)
     factor = jnp.minimum(1.0, 1.0 / jnp.sqrt(mean_sq + 1e-06))

time: 111 us -> 93 us (0.84)
  blocking collectives: 42.8 us -> 26 us
  local copies, waits for them, and re-layouts: 15.2 us -> 14 us
    psum x1 -> x0, blocking collectives: 30.4 us -> none  [per_device(): raw = lax.psum(partial_value, 'dp')]
    all_gather x0 -> x1, blocking collectives: none -> 13.6 us  [per_device(): raw = jnp.sum(lax.all_gather(partial_value, 'dp'), axis=0)]
    unnamed x18 -> x9, local copies, waits for them, and re-layouts: 8.56 us -> 7.15 us
  transfers between devices with their start and end apart: 3 -> 3, of which waited for: 2 -> 2; matrix products, arithmetic and copies ran while one was open for 8% -> 9% of each run, Pallas kernels for 0% -> 0%
where the time goes in v1:
time: 93 us; the launch traced here: 92.5 us
  blocking collectives  26 us (28%)
  waiting for transfers between devices  25.6 us (28%)
  local copies, waits for them, and re-layouts  14 us (15%)
  starting transfers between devices  12.6 us (14%)
  matrix products  10 us (11%)
  other arithmetic  2.77 us (3%)
  between operations  1.49 us (2%)
    all_gather x1, blocking collectives, per_device(): raw = jnp.sum(lax.all_gather(partial_value, 'dp'), axis=0)  13.6 us
    all_to_all x1, waiting for transfers between devices, per_device(): lax.all_to_all(cotangent, 'seq', split_axis=2, concat_axis=1, tiled=True)  13.5 us
    psum x1, blocking collectives, per_device(): total_sq = lax.psum(jnp.sum(raw * raw), 'seq')  12.4 us
    all_to_all x1, waiting for transfers between devices, per_device(): lax.all_to_all(tokens, 'seq', split_axis=2, concat_axis=1, tiled=True)  12.2 us
    unnamed x9, local copies, waits for them, and re-layouts  7.15 us
    all_to_all x1, starting transfers between devices, per_device(): lax.all_to_all(cotangent, 'seq', split_axis=2, concat_axis=1, tiled=True)  5.33 us
    all_to_all x1, starting transfers between devices, per_device(): lax.all_to_all(grad_cols, 'seq', split_axis=1, concat_axis=2, tiled=True)  3.74 us
    all_to_all x1, starting transfers between devices, per_device(): lax.all_to_all(tokens, 'seq', split_axis=2, concat_axis=1, tiled=True)  3.56 us
  transfers between devices with their start and end apart: 3, of which 2 were waited for; matrix products, arithmetic and copies ran while one was open for 9% of the time, Pallas kernels for 0%

profile of v1, /device:TPU:0, one launch (start us, length us, event | category | flops | bytes accessed | tf_op | source)
XLA Modules:
  0.0 92.5 jit_solution(5664738102535985116)
XLA Ops:
  0.6 0.0 copy-start
  0.6 3.6 %copy.64 = f32[1,128,2048]{1,0,2:T(1,128)} copy(f32[1,128,2048]{2,1,0:T(8,128)} %param.4) | data formatting | bytes 2097152 | tf_op args[1]
  4.3 0.0 copy-start.1
  4.3 5.3 %all-to-all-start.1 = ((f32[1,128,2048]{1,0,2:T(1,128)}), f32[1,128,2048]{1,0,2:T(1,128)S(1)}, u32[]{:S(2)}, u32[]{:S(2)}) async-start(f32[1,128,2048]{1,0,2:T(1,128)} %copy.64), calls=%async_computation.1 | async-start | bytes 2097152 | tf_op jit(solution)/shard_map/all_to_all | solution.py:44
  9.6 0.0 copy-done.1
  9.6 1.9 %copy.61 = f32[1,128,2048]{1,0,2:T(1,128)} copy(f32[1,128,2048]{2,1,0:T(8,128)S(1)} %copy-done.1) | data formatting | bytes 2097152 | tf_op args[0]
  11.5 13.5 %all-to-all-done.1 = f32[1,128,2048]{1,0,2:T(1,128)S(1)} async-done(((f32[1,128,2048]{1,0,2:T(1,128)}), f32[1,128,2048]{1,0,2:T(1,128)S(1)}, u32[]{:S(2)}, u32[]{:S(2)}) %all-to-all-start.1) | async-done | bytes 1048608 | tf_op jit(solution)/shard_map/all_to_all | solution.py:44
  25.0 3.6 %all-to-all-start = ((f32[1,128,2048]{1,0,2:T(1,128)}), f32[1,128,2048]{1,0,2:T(1,128)S(1)}, u32[]{:S(2)}, u32[]{:S(2)}) async-start(f32[1,128,2048]{1,0,2:T(1,128)} %copy.61), calls=%async_computation | async-start | bytes 2097152 | tf_op jit(solution)/shard_map/all_to_all | solution.py:43
  28.6 0.0 copy-done
  28.6 0.2 copy.83
  28.8 1.3 %copy.65 = f32[1,8,128,256]{3,2,1,0:T(8,128)} copy(f32[1,8,128,256]{2,3,1,0:T(8,128)S(1)} %bitcast.64) | data formatting | bytes 2097152 | tf_op jit(solution)/shard_map/all_to_all | solution.py:44
  30.1 1.5 %reduce_sum.46 = f32[128,256]{1,0:T(8,128)S(1)} reduce(f32[128,8,256]{2,1,0:T(8,128)} %bitcast.66, f32[]{:T(128)} %constant.6.clone.1), dimensions={1}, to_apply=%region_2.0 | reduce | flops 229376 | bytes 1179652 | tf_op jit(solution)/shard_map/reduce_sum | solution.py:53
  31.6 0.1 copy.66
  31.7 12.2 %all-to-all-done = f32[1,128,2048]{1,0,2:T(1,128)S(1)} async-done(((f32[1,128,2048]{1,0,2:T(1,128)}), f32[1,128,2048]{1,0,2:T(1,128)S(1)}, u32[]{:S(2)}, u32[]{:S(2)}) %all-to-all-start) | async-done | bytes 1048608 | tf_op jit(solution)/shard_map/all_to_all | solution.py:43
  43.9 0.3 copy.62
  44.2 0.6 copy.63
  44.8 1.8 %convolution_bitcast_fusion.2 = f32[3,1,128,256]{2,0,3,1:T(4,128)S(1)} fusion(f32[3,8,256]{1,0,2:T(4,128)S(1)} %copy.83, f32[128,8,256]{0,1,2:T(8,128)S(1)} %copy.63), kind=kOutput, calls=%fused_computation.2 | convolution fusion | flops 9437184 | bytes 1466368 | tf_op jit(solution)/shard_map/bjic,mic->mbjc/dot_general | solution.py:52
  46.6 0.3 fusion.8
  46.8 0.6 fusion.9
  47.4 0.1 fusion.1
  47.5 0.6 fusion.5
  48.1 0.6 multiply_reduce_fusion
  48.7 0.6 convolution_multiply_fusion.1
  49.4 0.4 convolution_multiply_fusion.2
  49.8 3.4 %convolution_bitcast_fusion = f32[1,128,8,256]{1,2,3,0:T(8,128)} fusion(f32[3,8,256]{1,0,2:T(4,128)S(1)} %copy.83, f32[1,1,128,256]{2,0,3,1:T(1,128)S(1)} %bitcast.75, f32[1,1,128,256]{2,0,3,1:T(1,128)S(1)} %bitcast.77, f32[1,1,128,256]{2,0,3,1:T(1,128)S(1)} %bitcast.79), kind=kOutput, calls=%fused_computation | convolution fusion | flops 9633792 | bytes 1466368 | tf_op jit(solution)/shard_map/mbjc,mic->bjic/dot_general | solution.py:56
  53.2 1.7 %copy.73 = f32[1,128,8,256]{3,2,1,0:T(8,128)S(1)} copy(f32[1,128,8,256]{1,2,3,0:T(8,128)} %convolution_bitcast_fusion) | data formatting | bytes 2097152 | tf_op jit(solution)/shard_map/mbjc,mic->bjic/transpose | solution.py:56
  54.9 2.0 %copy.74 = f32[1,1024,256]{2,0,1:T(1,128)} copy(f32[1,1024,256]{2,1,0:T(8,128)S(1)} %bitcast.68) | data formatting | bytes 2097152 | tf_op jit(solution)/shard_map/reshape | solution.py:56
  57.0 3.7 %all-to-all-start.2 = ((f32[1,1024,256]{2,0,1:T(1,128)}), f32[1,1024,256]{2,0,1:T(1,128)S(1)}, u32[]{:S(2)}, u32[]{:S(2)}) async-start(f32[1,1024,256]{2,0,1:T(1,128)} %copy.74), calls=%async_computation.2 | async-start | bytes 2097152 | tf_op jit(solution)/shard_map/all_to_all | solution.py:59
  60.7 2.0 %convolution_bitcast_fusion.1 = f32[3,8,256]{1,0,2:T(4,128)S(1)} fusion(f32[128,8,256]{0,1,2:T(8,128)S(1)} %copy.63, f32[1,1,128,256]{2,0,3,1:T(1,128)S(1)} %bitcast.76, f32[1,1,128,256]{2,0,3,1:T(1,128)S(1)} %bitcast.78, f32[1,1,128,256]{2,0,3,1:T(1,128)S(1)} %bitcast.80), kind=kOutput, calls=%fused_computation.1 | convolution fusion | flops 9633792 | bytes 1466368 | tf_op jit(solution)/shard_map/mbjc,bjic->mic/dot_general | solution.py:60
  62.7 0.1 copy.77
  62.9 13.6 %all-gather = f32[12,8,256]{2,1,0:T(8,128)S(1)} all-gather(f32[3,8,256]{2,1,0:T(8,128)S(1)} %copy.77), channel_id=2, replica_groups=mesh['dp'=4,'seq'=8] {'dp'}, dimensions={0}, use_global_device_ids=true | all-gather | bytes 122880 | tf_op jit(solution)/shard_map/all_gather | solution.py:61
  76.5 0.6 multiply_reduce_fusion.1
  77.1 12.4 %psum.7 = f32[]{:T(128)} all-reduce(f32[]{:T(128)} %multiply_reduce_fusion.1), channel_id=1, replica_groups=mesh['dp'=4,'seq'=8] {'seq'}, use_global_device_ids=true, to_apply=%region_6.0 | all-reduce | flops 1 | bytes 8 | tf_op jit(solution)/shard_map/psum | solution.py:62
  90.2 0.6 broadcast_multiply_fusion
  90.8 0.0 all-to-all-done.2
  90.8 0.1 copy.82
  90.9 0.3 copy.75
  91.2 1.3 %copy.78 = f32[1,128,2048]{2,1,0:T(8,128)} copy(f32[1,128,2048]{1,2,0:T(8,128)S(1)} %bitcast.70) | data formatting | bytes 2097152
  (2 shorter events, 0.0 us)
Async XLA Ops:
  0.6 27.9 %copy-start = (f32[3,8,2048]{2,1,0:T(8,128)S(1)}, f32[3,8,2048]{2,1,0:T(8,128)}, u32[]{:S(2)}) copy-start(f32[3,8,2048]{2,1,0:T(8,128)} %param.5) | copy-start | bytes 589828
  4.3 5.3 %copy-start.1 = (f32[1,128,2048]{2,1,0:T(8,128)S(1)}, f32[1,128,2048]{2,1,0:T(8,128)}, u32[]{:S(2)}) copy-start(f32[1,128,2048]{2,1,0:T(8,128)} %param.3) | copy-start | bytes 3145732
  4.3 20.7 %all-to-all-start.1 = ((f32[1,128,2048]{1,0,2:T(1,128)}), f32[1,128,2048]{1,0,2:T(1,128)S(1)}, u32[]{:S(2)}, u32[]{:S(2)}) async-start(f32[1,128,2048]{1,0,2:T(1,128)} %copy.64), calls=%async_computation.1 | async-start | bytes 2097152 | tf_op jit(solution)/shard_map/all_to_all | solution.py:44
  25.0 18.9 %all-to-all-start = ((f32[1,128,2048]{1,0,2:T(1,128)}), f32[1,128,2048]{1,0,2:T(1,128)S(1)}, u32[]{:S(2)}, u32[]{:S(2)}) async-start(f32[1,128,2048]{1,0,2:T(1,128)} %copy.61), calls=%async_computation | async-start | bytes 2097152 | tf_op jit(solution)/shard_map/all_to_all | solution.py:43
  57.0 33.8 %all-to-all-start.2 = ((f32[1,1024,256]{2,0,1:T(1,128)}), f32[1,1024,256]{2,0,1:T(1,128)S(1)}, u32[]{:S(2)}, u32[]{:S(2)}) async-start(f32[1,1024,256]{2,0,1:T(1,128)} %copy.74), calls=%async_computation.2 | async-start | bytes 2097152 | tf_op jit(solution)/shard_map/all_to_all | solution.py:59
